TPU v7x, 32 devices: a whole 2x2x4 slice. The times are simulated.
32 devices in a mesh: subtree: 4 (over y, core), tile: 8 (over z, x).
Axes of the slice: x: 2, y: 2, z: 4, core: 2. Of those that a mesh axis runs over, the one named last changes fastest.
Arguments:
- interface_stiffness: float32 [4, 4096, 4096], P('subtree', 'tile'), may hold values from -3 to 3
- lower_factor: bfloat16 [4, 4096, 512], P('subtree', 'tile'), may hold values from -0.25 to 0.25
- upper_factor: bfloat16 [4, 512, 4096], P('subtree', None, 'tile'), may hold values from -6 to 6
- modes: bfloat16 [4096, 256], P('tile'), may hold values from -0.09375 to 0.09375
- gyro_rows: int32 [512], replicated, may hold values from 0 to 4095, as said below
- gyro_coupling: float32 [512, 512], replicated, may hold values from -24 to 24
- spin_softening: float32 [512], replicated, may hold values from 0.5 to 8
- speed_index: int32 [2], replicated, may hold values from 0 to 63
Outputs:
- schur: float32 [4096, 4096], P('tile', 'subtree')
- campbell: float32 [2, 256, 256], P(None, 'tile', 'subtree')
Inputs may be any that keep to these rules, and one draw needn't show every extreme that they name: `gyro_rows`: distinct interface degrees of freedom, in whole aligned blocks of 8 consecutive ones.
All inputs are finite; a program needn't handle non-finite values.
Results may differ from a plain program's by a relative error of at most 0.0003.
Values may be sent and summed in bfloat16 or wider, within the bound.
No kernel may reach another device: no remote copies, remote signals or barrier semaphores. Data moves between devices by JAX's collectives and lax.ppermute only.
A program may use at most 64 MiB of HBM per device.

v0:
```python
import jax
import jax.numpy as jnp
from jax import lax
from jax.sharding import PartitionSpec as P

SPEED_STEPS = 64
OMEGA_TOP = 2.0


def partner(block, axis, distance):
    count = lax.axis_size(axis)
    route = []
    for low in range(count):
        high = low | 1 << distance
        if high != low and high < count:
            route += [(low, high), (high, low)]
    return lax.ppermute(block, axis, route)


def shards(
    interface_stiffness,
    lower_factor,
    upper_factor,
    modes,
    gyro_rows,
    gyro_coupling,
    spin_softening,
    speed_index,
):
    tile_count = lax.axis_size("tile")
    branch_count = lax.axis_size("subtree")
    tile_pos = lax.axis_index("tile")
    branch_pos = lax.axis_index("subtree")
    mode_count = modes.shape[1]
    mode_cols = mode_count // branch_count
    mode_rows_dev = mode_count // tile_count
    coupled = jnp.einsum(
        "lrk,lkn->rn",
        lower_factor,
        lax.all_gather(upper_factor, "tile", axis=2, tiled=True),
        preferred_element_type=jnp.float32,
    )
    schur_rows = jnp.sum(interface_stiffness, axis=0) - coupled
    full_width = schur_rows.shape[1]
    own_width = full_width // branch_count
    own_first = branch_pos * own_width
    schur_part = schur_rows
    for level_bit in range(branch_count.bit_length() - 1):
        schur_part = schur_part + partner(schur_part, "subtree", level_bit)
    schur_out = lax.dynamic_slice_in_dim(schur_part, own_first, own_width, 1)
    col_first = branch_pos * mode_cols
    segment = lax.all_gather(modes, "tile", axis=0, tiled=True)
    row_count = segment.shape[0]
    wanted = lax.dynamic_slice_in_dim(segment, col_first, mode_cols, 1).astype(jnp.float32)
    response = jnp.dot(
        schur_part, wanted, precision=lax.Precision.HIGHEST, preferred_element_type=jnp.float32
    )
    inside = (gyro_rows >= 0) & (gyro_rows < row_count)
    taken = jnp.take(segment, jnp.clip(gyro_rows, 0, row_count - 1), axis=0).astype(jnp.float32)
    picked = jnp.where(inside[:, None], taken, jnp.float32(0.0))
    response, picked = (response, picked)
    local_modes = modes.astype(jnp.float32)
    partial_value = jnp.einsum(
        "rm,rc->mc",
        local_modes,
        response,
        precision=lax.Precision.HIGHEST,
        preferred_element_type=jnp.float32,
    )
    stiff_block = lax.psum_scatter(partial_value, "tile", scatter_dimension=0, tiled=True)
    skew_part = 0.5 * (gyro_coupling - gyro_coupling.T)
    left_modes = lax.dynamic_slice_in_dim(picked, tile_pos * mode_rows_dev, mode_rows_dev, 1)
    right_modes = lax.dynamic_slice_in_dim(picked, branch_pos * mode_cols, mode_cols, 1)
    turned = jnp.dot(
        skew_part, right_modes, precision=lax.Precision.HIGHEST, preferred_element_type=jnp.float32
    )
    gyro_block = jnp.einsum(
        "gm,gc->mc",
        left_modes,
        turned,
        precision=lax.Precision.HIGHEST,
        preferred_element_type=jnp.float32,
    )
    spin_block = jnp.einsum(
        "gm,gc->mc",
        left_modes,
        spin_softening[:, None] * right_modes,
        precision=lax.Precision.HIGHEST,
        preferred_element_type=jnp.float32,
    )
    speeds_omega = OMEGA_TOP * (speed_index.astype(jnp.float32) + 1.0) / SPEED_STEPS
    campbell = (
        stiff_block[None]
        + speeds_omega[:, None, None] * gyro_block[None]
        - (speeds_omega * speeds_omega)[:, None, None] * spin_block[None]
    )
    return (schur_out, campbell)


def solution(mesh):
    placed = (
        P("subtree", "tile", None),
        P("subtree", "tile", None),
        P("subtree", None, "tile"),
        P("tile", None),
        P(),
        P(),
        P(),
        P(),
    )
    return jax.shard_map(
        shards,
        mesh=mesh,
        in_specs=placed,
        out_specs=(P("tile", "subtree"), P(None, "tile", "subtree")),
        check_vma=False,
    )
```

profile of v0, /device:TPU:0, one launch (start us, length us, event | category | flops | bytes accessed | tf_op | source)
XLA Modules:
  0.0 391.6 jit_solution(2700897672948704366)
XLA Ops:
  7.2 0.0 copy-start
  7.2 0.0 all-gather.3.cloned.1.call-start
  7.2 0.7 all-gather.3.cloned.1.call-update
  7.9 0.0 all-gather.5.cloned.1.call-start
  8.0 79.8 %all-gather.3.cloned.1.call-done = bf16[1,512,4096]{2,1,0:T(8,128)(2,1)} async-done(((bf16[1,512,512]{2,1,0:T(8,128)(2,1)}), bf16[1,512,4096]{2,1,0:T(8,128)(2,1)}) %all-gather.3.cloned.1.call-update) | async-done | bytes 4194320 | tf_op jit(solution)/shard_map/all_gather | solution.py:40
  87.8 0.0 copy-done
  87.8 7.0 %bitcast_subtract_fusion = f32[512,4096]{1,0:T(8,128)S(1)} fusion(f32[1,512,4096]{2,1,0:T(8,128)} %param.8, bf16[1,512,4096]{2,1,0:T(8,128)(2,1)} %all-gather.3.cloned.1.call-done, bf16[1,512,512]{2,1,0:T(8,128)(2,1)S(1)} %copy-done), kind=kOutput, calls=%fused_computation.1 | convolution fusion | flops 2149580800 | bytes 21495808 | tf_op jit(solution)/shard_map/lrk,lkn->rn/dot_general | solution.py:37
  94.8 0.0 copy-start.1
  94.8 3.2 copy-done.1
  98.1 0.0 copy-start.3
  98.1 0.0 copy-start.5
  98.1 0.0 copy-start.7
  98.1 0.0 copy-start.6
  98.1 0.1 collective-permute-start
  98.2 13.3 %collective-permute-done = f32[512,4096]{1,0:T(8,128)} collective-permute-done((f32[512,4096]{1,0:T(8,128)S(1)}, f32[512,4096]{1,0:T(8,128)}, u32[]{:S(2)}, u32[]{:S(2)}) %collective-permute-start) | collective-permute-done | bytes 8388640 | tf_op jit(solution)/shard_map/ppermute | solution.py:17
  111.4 11.1 %add.35 = f32[512,4096]{1,0:T(8,128)} add(f32[512,4096]{1,0:T(8,128)} %copy-done.1, f32[512,4096]{1,0:T(8,128)} %collective-permute-done) | non-fusion elementwise | flops 2097152 | bytes 25165824 | tf_op jit(solution)/shard_map/add | solution.py:49
  122.6 1.5 collective-permute-start.1
  124.1 0.0 all-gather.5.cloned.1.call-update
  124.1 0.0 reduce-scatter.4.cloned.1.call-start
  124.1 0.0 copy-done.3
  124.2 0.3 copy.13
  124.5 0.0 copy-done.5
  124.5 0.0 copy-done.7
  124.6 46.2 %all-gather.5.cloned.1.call-done = bf16[4096,256]{1,0:T(8,128)(2,1)} async-done(((bf16[512,256]{1,0:T(8,128)(2,1)}), bf16[4096,256]{1,0:T(8,128)(2,1)}) %all-gather.5.cloned.1.call-update) | async-done | bytes 2097168 | tf_op jit(solution)/shard_map/all_gather | solution.py:52
  170.8 3.4 gather_fusion
  174.2 0.2 convert_select_fusion
  174.4 0.0 copy-done.6
  174.4 0.8 fusion.8
  175.3 1.1 fusion.2
  176.4 0.7 fusion.13
  177.0 0.0 copy-start.2
  177.0 128.3 %collective-permute-done.1 = f32[512,4096]{1,0:T(8,128)} collective-permute-done((f32[512,4096]{1,0:T(8,128)}, f32[512,4096]{1,0:T(8,128)}, u32[]{:S(2)}, u32[]{:S(2)}) %collective-permute-start.1) | collective-permute-done | bytes 8388640 | tf_op jit(solution)/shard_map/ppermute | solution.py:17
  305.4 11.1 %add.36 = f32[512,4096]{1,0:T(8,128)} add(f32[512,4096]{1,0:T(8,128)} %add.35, f32[512,4096]{1,0:T(8,128)} %collective-permute-done.1) | non-fusion elementwise | flops 2097152 | bytes 25165824 | tf_op jit(solution)/shard_map/add | solution.py:49
  316.5 0.0 copy-done.2
  316.5 0.0 copy-start.4
  316.5 6.7 %fusion.4 = f32[512,64]{1,0:T(8,128)S(1)} fusion(f32[512,4096]{1,0:T(8,128)} %add.36, bf16[4096,256]{1,0:T(8,128)(2,1)S(1)} %copy-done.2, s32[]{:T(128)S(6)} %select_n.24), kind=kOutput, calls=%fused_computation.7 | convolution fusion | flops 1610612736 | bytes 9568260 | tf_op jit(solution)/shard_map/dot_general | solution.py:55
  323.3 0.0 copy-done.4
  323.3 0.4 convolution_bitcast_fusion
  323.6 0.8 copy.14
  324.4 0.0 reduce-scatter.4.cloned.1.call-update
  324.4 3.2 constant_dynamic-slice_fusion
  327.6 56.0 %reduce-scatter.4.cloned.1.call-done = f32[32,64]{1,0:T(8,128)} async-done(((f32[256,64]{1,0:T(8,128)}), f32[32,64]{1,0:T(8,128)}) %reduce-scatter.4.cloned.1.call-update) | async-done | bytes 8208 | tf_op jit(solution)/shard_map/reduce_scatter | solution.py:70
  383.6 1.4 multiply_subtract_fusion
  (4 shorter events, 0.0 us)
Async XLA Ops:
  7.2 80.6 %copy-start = (bf16[1,512,512]{2,1,0:T(8,128)(2,1)S(1)}, bf16[1,512,512]{2,1,0:T(8,128)(2,1)}, u32[]{:S(2)}) copy-start(bf16[1,512,512]{2,1,0:T(8,128)(2,1)} %param.9) | copy-start | bytes 1572868
  7.2 80.6 %all-gather.3.cloned.1.call-start = ((), (), s32[]{:S(2)}) async-start(), calls=%async_computation.1 | async-start | bytes 4718592 | tf_op jit(solution)/shard_map/all_gather | solution.py:40
  7.9 162.9 %all-gather.5.cloned.1.call-start = ((), (), s32[]{:S(2)}) async-start(), calls=%async_computation.2 | async-start | bytes 2359296 | tf_op jit(solution)/shard_map/all_gather | solution.py:52
  94.8 3.2 copy-start.1
  98.1 26.1 %copy-start.3 = (f32[512,512]{1,0:T(8,128)S(1)}, f32[512,512]{1,0:T(8,128)}, u32[]{:S(2)}) copy-start(f32[512,512]{1,0:T(8,128)} %param.13) | copy-start | bytes 3145732
  98.1 26.4 %copy-start.5 = (s32[512]{0:T(512)S(1)}, s32[512]{0:T(512)}, u32[]{:S(2)}) copy-start(s32[512]{0:T(512)} %param.12) | copy-start | bytes 6148
  98.1 26.5 %copy-start.7 = (s32[2]{0:T(128)S(1)}, s32[2]{0:T(128)}, u32[]{:S(2)}) copy-start(s32[2]{0:T(128)} %param.15) | copy-start | bytes 28
  98.1 76.4 %copy-start.6 = (f32[512]{0:T(512)S(1)}, f32[512]{0:T(512)}, u32[]{:S(2)}) copy-start(f32[512]{0:T(512)} %param.14) | copy-start | bytes 6148
  98.1 13.4 %collective-permute-start = (f32[512,4096]{1,0:T(8,128)S(1)}, f32[512,4096]{1,0:T(8,128)}, u32[]{:S(2)}, u32[]{:S(2)}) collective-permute-start(f32[512,4096]{1,0:T(8,128)S(1)} %bitcast_subtract_fusion), channel_id=1, source_target_pairs={{0,8},{8,0},{16,24},{24,16},{1,9},{9,1},{17,25},{25,17},{2,10},{10... | collective-permute-start | bytes 25165832 | tf_op jit(solution)/shard_map/ppermute | solution.py:17
  122.6 182.8 %collective-permute-start.1 = (f32[512,4096]{1,0:T(8,128)}, f32[512,4096]{1,0:T(8,128)}, u32[]{:S(2)}, u32[]{:S(2)}) collective-permute-start(f32[512,4096]{1,0:T(8,128)} %add.35), channel_id=1, source_target_pairs={{0,16},{16,0},{8,24},{24,8},{1,17},{17,1},{9,25},{25,9},{2,18},{18... | collective-permute-start | bytes 25165832 | tf_op jit(solution)/shard_map/ppermute | solution.py:17
  124.1 259.5 %reduce-scatter.4.cloned.1.call-start = ((), (), s32[]{:S(2)}) async-start(), calls=%async_computation.3 | async-start | bytes 147456 | tf_op jit(solution)/shard_map/reduce_scatter | solution.py:70
  177.0 139.5 %copy-start.2 = (bf16[4096,256]{1,0:T(8,128)(2,1)S(1)}, bf16[4096,256]{1,0:T(8,128)(2,1)}, u32[]{:S(2)}) copy-start(bf16[4096,256]{1,0:T(8,128)(2,1)} %all-gather.5.cloned.1.call-done) | copy-start | bytes 6291460
  316.5 6.7 %copy-start.4 = (bf16[512,256]{1,0:T(8,128)(2,1)S(1)}, bf16[512,256]{1,0:T(8,128)(2,1)}, u32[]{:S(2)}) copy-start(bf16[512,256]{1,0:T(8,128)(2,1)} %param.11) | copy-start | bytes 786436
Sparse Core Ops, SparseCore 0:
  10.1 77.7 all-gather.2
  124.2 46.5 all-gather.4
  324.5 59.0 reduce-scatter.3
where the time goes:
time: 392 us
  waiting for transfers between devices  324 us (83%)
  other arithmetic  23.9 us (6%)
  matrix products  16.7 us (4%)
  between operations  13.9 us (4%)
  local copies, waits for them, and re-layouts  10.9 us (3%)
    ppermute x2, waiting for transfers between devices, partner(): return lax.ppermute(block, axis, route)  142 us
    all_gather x1, waiting for transfers between devices, shards(): lax.all_gather(upper_factor, 'tile', axis=2, tiled=True)  79.8 us
    reduce_scatter x1, waiting for transfers between devices, shards(): lax.psum_scatter(partial_value, 'tile', scatter_dimension=0, tiled=True)  56 us
    all_gather x1, waiting for transfers between devices, shards(): segment = lax.all_gather(modes, 'tile', axis=0, tiled=True)  46.2 us
    add x2, other arithmetic, shards(): schur_part = schur_part + partner(schur_part, 'subtree', level_bit)  22.3 us
  transfers between devices with their start and end apart: 5, of which 5 were waited for; matrix products, arithmetic and copies ran while one was open for 2% of the time, Pallas kernels for 0%

commit v1 on v0

--- a/solution.py
+++ b/solution.py
@@ -34,12 +34,23 @@
     mode_count = modes.shape[1]
     mode_cols = mode_count // branch_count
     mode_rows_dev = mode_count // tile_count
-    coupled = jnp.einsum(
-        "lrk,lkn->rn",
-        lower_factor,
-        lax.all_gather(upper_factor, "tile", axis=2, tiled=True),
-        preferred_element_type=jnp.float32,
-    )
+    ways, here, hop = (lax.axis_size("tile"), lax.axis_index("tile"), upper_factor.shape[2])
+    earlier, later = ([], [])
+    going_up = going_down = upper_factor
+    for far in range(ways // 2 + 1):
+        earlier.append(
+            jnp.einsum("lrk,lkn->rn", lower_factor, going_up, preferred_element_type=jnp.float32)
+        )
+        if 0 < far < ways - ways // 2:
+            later.append(
+                jnp.einsum(
+                    "lrk,lkn->rn", lower_factor, going_down, preferred_element_type=jnp.float32
+                )
+            )
+        going_up = lax.ppermute(going_up, "tile", [(d, (d + 1) % ways) for d in range(ways)])
+        going_down = lax.ppermute(going_down, "tile", [(d, (d - 1) % ways) for d in range(ways)])
+    line = jnp.concatenate([*earlier[::-1], *later], axis=1)
+    coupled = jnp.roll(line, (here - ways // 2) * earlier[0].shape[1], axis=1)
     schur_rows = jnp.sum(interface_stiffness, axis=0) - coupled
     full_width = schur_rows.shape[1]
     own_width = full_width // branch_count

time: 392 us -> 427 us (1.089)
  waiting for transfers between devices: 324 us -> 292 us
  starting transfers between devices: 1.67 us -> 30.5 us
  local copies, waits for them, and re-layouts: 10.9 us -> 26.8 us
  matrix products: 16.7 us -> 28.1 us
  other arithmetic: 23.9 us -> 35 us
    all_gather x1 -> x0, waiting for transfers between devices: 79.8 us -> none  [shards(): lax.all_gather(upper_factor, 'tile', axis=2, tiled=True)]
    ppermute x0 -> x7, waiting for transfers between devices: none -> 49.8 us  [the longest x4 49.8 us: shards(): lax.ppermute(going_up, 'tile', [(d, (d + 1) % ways) for d in range(ways)])]
    ppermute x0 -> x7, starting transfers between devices: none -> 29.6 us  [the longest x3 21.5 us: shards(): lax.ppermute(going_down, 'tile', [(d, (d - 1) % ways) for d in range(ways)])]
    unnamed x18 -> x29, local copies, waits for them, and re-layouts: 4.35 us -> 20.4 us
    sub x0 -> x1, other arithmetic: none -> 11.1 us  [shards(): schur_rows = jnp.sum(interface_stiffness, axis=0) - coupled]
    dot_general x1 -> x8, matrix products: 7.01 us -> 13.9 us  [the longest x5 9.44 us: shards(): jnp.einsum('lrk,lkn->rn', lower_factor, going_up, preferred_element_type=...]
  transfers between devices with their start and end apart: 5 -> 11, of which waited for: 5 -> 8; matrix products, arithmetic and copies ran while one was open for 2% -> 8% of each run, Pallas kernels for 0% -> 0%
where the time goes in v1:
time: 427 us; the launch traced here: 426 us
  waiting for transfers between devices  292 us (68%)
  other arithmetic  35 us (8%)
  starting transfers between devices  30.5 us (7%)
  matrix products  28.1 us (7%)
  local copies, waits for them, and re-layouts  26.8 us (6%)
  between operations  14.2 us (3%)
    ppermute x2, waiting for transfers between devices, partner(): return lax.ppermute(block, axis, route)  139 us
    reduce_scatter x1, waiting for transfers between devices, shards(): lax.psum_scatter(partial_value, 'tile', scatter_dimension=0, tiled=True)  55.8 us
    ppermute x4, waiting for transfers between devices, shards(): lax.ppermute(going_up, 'tile', [(d, (d + 1) % ways) for d in range(ways)])  49.8 us
    all_gather x1, waiting for transfers between devices, shards(): segment = lax.all_gather(modes, 'tile', axis=0, tiled=True)  47 us
    add x2, other arithmetic, shards(): schur_part = schur_part + partner(schur_part, 'subtree', level_bit)  22.3 us
    ppermute x3, starting transfers between devices, shards(): lax.ppermute(going_down, 'tile', [(d, (d - 1) % ways) for d in range(ways)])  21.5 us
    unnamed x29, local copies, waits for them, and re-layouts  20.4 us
    sub x1, other arithmetic, shards(): schur_rows = jnp.sum(interface_stiffness, axis=0) - coupled  11.1 us
  transfers between devices with their start and end apart: 11, of which 8 were waited for; matrix products, arithmetic and copies ran while one was open for 8% of the time, Pallas kernels for 0%

profile of v1, /device:TPU:0, one launch (start us, length us, event | category | flops | bytes accessed | tf_op | source)
XLA Modules:
  0.0 426.3 jit_solution(1703646700395421836)
XLA Ops:
  7.2 0.0 copy-start
  7.2 0.0 copy-start.5
  7.2 0.0 all-gather.2.cloned.1.call-start
  7.2 3.0 collective-permute-start
  10.2 15.2 %collective-permute-done = bf16[1,512,512]{2,1,0:T(8,128)(2,1)S(1)} collective-permute-done((bf16[1,512,512]{2,1,0:T(8,128)(2,1)}, bf16[1,512,512]{2,1,0:T(8,128)(2,1)S(1)}, u32[]{:S(2)}, u32[]{:S(2)}) %collective-permute-start) | collective-permute-done | bytes 524320 | tf_op jit(solution)/shard_map/ppermute | solution.py:50
  25.4 0.0 collective-permute-start.1
  25.4 4.7 %collective-permute-start.4 = (bf16[1,512,512]{2,1,0:T(8,128)(2,1)}, bf16[1,512,512]{2,1,0:T(8,128)(2,1)S(1)}, u32[]{:S(2)}, u32[]{:S(2)}) collective-permute-start(bf16[1,512,512]{2,1,0:T(8,128)(2,1)} %param.10), channel_id=1, source_target_pairs={{0,7},{1,0},{2,1},{3,2},{4,3},{5,4},{6,5},{7,6},{8,15},{9,8},{10,9... | collective-permute-start | bytes 1572872 | tf_op jit(solution)/shard_map/ppermute | solution.py:51
  30.1 17.4 %collective-permute-done.1 = bf16[1,512,512]{2,1,0:T(8,128)(2,1)S(1)} collective-permute-done((bf16[1,512,512]{2,1,0:T(8,128)(2,1)S(1)}, bf16[1,512,512]{2,1,0:T(8,128)(2,1)S(1)}, u32[]{:S(2)}, u32[]{:S(2)}) %collective-permute-start.1) | collective-permute-done | bytes 524320 | tf_op jit(solution)/shard_map/ppermute | solution.py:50
  47.5 2.5 collective-permute-start.2
  50.0 0.0 collective-permute-done.4
  50.0 12.3 %collective-permute-start.5 = (bf16[1,512,512]{2,1,0:T(8,128)(2,1)S(1)}, bf16[1,512,512]{2,1,0:T(8,128)(2,1)S(1)}, u32[]{:S(2)}, u32[]{:S(2)}) collective-permute-start(bf16[1,512,512]{2,1,0:T(8,128)(2,1)S(1)} %collective-permute-done.4), channel_id=1, source_target_pairs={{0,7},{1,0},{2,1},{3,2},{4,3},{5,4},{6,5},{7,6},{8,15},{9,8},{10,9... | collective-permute-start | bytes 1572872 | tf_op jit(solution)/shard_map/ppermute | solution.py:51
  62.4 8.9 %collective-permute-done.2 = bf16[1,512,512]{2,1,0:T(8,128)(2,1)} collective-permute-done((bf16[1,512,512]{2,1,0:T(8,128)(2,1)S(1)}, bf16[1,512,512]{2,1,0:T(8,128)(2,1)}, u32[]{:S(2)}, u32[]{:S(2)}) %collective-permute-start.2) | collective-permute-done | bytes 524320 | tf_op jit(solution)/shard_map/ppermute | solution.py:50
  71.3 2.6 collective-permute-start.3
  73.9 9.0 %copy.14 = f32[1,512,4096]{1,2,0:T(8,128)} copy(f32[1,512,4096]{2,1,0:T(8,128)} %param.8) | data formatting | bytes 16777216 | tf_op args[0]
  82.9 0.0 collective-permute-done.5
  82.9 4.5 %collective-permute-start.6 = (bf16[1,512,512]{2,1,0:T(8,128)(2,1)S(1)}, bf16[1,512,512]{2,1,0:T(8,128)(2,1)S(1)}, u32[]{:S(2)}, u32[]{:S(2)}) collective-permute-start(bf16[1,512,512]{2,1,0:T(8,128)(2,1)S(1)} %collective-permute-done.5), channel_id=1, source_target_pairs={{0,7},{1,0},{2,1},{3,2},{4,3},{5,4},{6,5},{7,6},{8,15},{9,8},{10,9... | collective-permute-start | bytes 1572872 | tf_op jit(solution)/shard_map/ppermute | solution.py:51
  87.3 8.3 %collective-permute-done.3 = bf16[1,512,512]{2,1,0:T(8,128)(2,1)} collective-permute-done((bf16[1,512,512]{2,1,0:T(8,128)(2,1)}, bf16[1,512,512]{2,1,0:T(8,128)(2,1)}, u32[]{:S(2)}, u32[]{:S(2)}) %collective-permute-start.3) | collective-permute-done | bytes 524320 | tf_op jit(solution)/shard_map/ppermute | solution.py:50
  95.6 0.0 copy-done
  95.6 2.5 constant_dynamic-update-slice_fusion.15
  98.2 2.5 constant_dynamic-update-slice_fusion.14
  100.7 1.5 constant_dynamic-update-slice_fusion.13
  102.1 1.4 constant_dynamic-update-slice_fusion.12
  103.6 0.0 copy-done.5
  103.6 1.5 constant_dynamic-update-slice_fusion.11
  105.1 1.5 constant_dynamic-update-slice_fusion.10
  106.6 1.5 constant_dynamic-update-slice_fusion.9
  108.0 0.0 collective-permute-done.6
  108.0 1.6 constant_dynamic-update-slice_fusion.8
  109.6 1.1 constant_dynamic-update-slice_fusion.7
  110.7 1.1 constant_dynamic-update-slice_fusion.6
  111.8 1.0 constant_dynamic-update-slice_fusion.5
  112.8 1.1 constant_dynamic-update-slice_fusion.4
  113.9 1.1 constant_dynamic-update-slice_fusion.3
  114.9 1.0 constant_dynamic-update-slice_fusion.2
  116.0 1.1 constant_dynamic-update-slice_fusion.1
  117.1 1.1 constant_dynamic-update-slice_fusion
  118.1 11.1 %bitcast_subtract_fusion = f32[512,4096]{0,1:T(8,128)} fusion(f32[1,512,4096]{1,2,0:T(8,128)} %copy.14, f32[512,8192]{0,1:T(8,128)} %constant_dynamic-update-slice_fusion, s32[]{:T(128)S(6)} %select_n.37), kind=kLoop, calls=%fused_computation.1 | loop fusion | flops 2097152 | bytes 25165828 | tf_op jit(solution)/shard_map/sub | solution.py:54
  129.3 0.1 collective-permute-start.7
  129.3 13.5 %collective-permute-done.7 = f32[512,4096]{0,1:T(8,128)} collective-permute-done((f32[512,4096]{0,1:T(8,128)}, f32[512,4096]{0,1:T(8,128)}, u32[]{:S(2)}, u32[]{:S(2)}) %collective-permute-start.7) | collective-permute-done | bytes 8388640 | tf_op jit(solution)/shard_map/ppermute | solution.py:17
  142.8 11.1 %add.48 = f32[512,4096]{0,1:T(8,128)} add(f32[512,4096]{0,1:T(8,128)} %bitcast_subtract_fusion, f32[512,4096]{0,1:T(8,128)} %collective-permute-done.7) | non-fusion elementwise | flops 2097152 | bytes 25165824 | tf_op jit(solution)/shard_map/add | solution.py:60
  154.0 0.6 collective-permute-start.8
  154.6 0.0 all-gather.2.cloned.1.call-update
  154.6 0.2 reduce-scatter.4.cloned.1.call-start
  154.9 0.0 copy-done.3
  154.9 1.3 copy.16
  156.2 0.0 copy-done.6
  156.2 47.0 %all-gather.2.cloned.1.call-done = bf16[4096,256]{1,0:T(8,128)(2,1)} async-done(((bf16[512,256]{1,0:T(8,128)(2,1)}), bf16[4096,256]{1,0:T(8,128)(2,1)}) %all-gather.2.cloned.1.call-update) | async-done | bytes 2097168 | tf_op jit(solution)/shard_map/all_gather | solution.py:63
  203.2 3.6 gather_fusion
  206.8 0.2 convert_select_fusion
  207.0 0.8 fusion.30
  207.8 2.6 fusion.1
  210.5 0.0 copy-start.1
  210.5 0.7 fusion.35
  211.1 125.6 %collective-permute-done.8 = f32[512,4096]{0,1:T(8,128)} collective-permute-done((f32[512,4096]{0,1:T(8,128)}, f32[512,4096]{0,1:T(8,128)}, u32[]{:S(2)}, u32[]{:S(2)}) %collective-permute-start.8) | collective-permute-done | bytes 8388640 | tf_op jit(solution)/shard_map/ppermute | solution.py:17
  336.8 11.1 %add.49 = f32[512,4096]{0,1:T(8,128)} add(f32[512,4096]{0,1:T(8,128)} %add.48, f32[512,4096]{0,1:T(8,128)} %collective-permute-done.8) | non-fusion elementwise | flops 2097152 | bytes 25165824 | tf_op jit(solution)/shard_map/add | solution.py:60
  347.9 9.6 %fusion.3 = f32[512,64]{1,0:T(8,128)S(1)} fusion(f32[512,4096]{0,1:T(8,128)} %add.49, bf16[4096,256]{1,0:T(8,128)(2,1)S(1)} %copy-done.2, s32[]{:T(128)S(6)} %select_n.39), kind=kOutput, calls=%fused_computation.6 | convolution fusion | flops 1610612736 | bytes 9568260 | tf_op jit(solution)/shard_map/dot_general | solution.py:66
  357.6 0.0 copy-done.4
  357.6 0.4 convolution_bitcast_fusion
  357.9 0.8 copy.18
  358.7 0.0 reduce-scatter.4.cloned.1.call-update
  358.7 1.8 constant_dynamic-slice_fusion
  360.5 1.8 copy.17
  362.3 55.8 %reduce-scatter.4.cloned.1.call-done = f32[32,64]{1,0:T(8,128)} async-done(((f32[256,64]{1,0:T(8,128)}), f32[32,64]{1,0:T(8,128)}) %reduce-scatter.4.cloned.1.call-update) | async-done | bytes 8208 | tf_op jit(solution)/shard_map/reduce_scatter | solution.py:81
  418.1 1.4 multiply_subtract_fusion
  (14 shorter events, 0.0 us)
Async XLA Ops:
  7.2 88.5 %copy-start = (bf16[1,512,512]{2,1,0:T(8,128)(2,1)S(1)}, bf16[1,512,512]{2,1,0:T(8,128)(2,1)}, u32[]{:S(2)}) copy-start(bf16[1,512,512]{2,1,0:T(8,128)(2,1)} %param.9) | copy-start | bytes 1572868
  7.2 96.4 %copy-start.5 = (bf16[1,512,512]{2,1,0:T(8,128)(2,1)S(1)}, bf16[1,512,512]{2,1,0:T(8,128)(2,1)}, u32[]{:S(2)}) copy-start(bf16[1,512,512]{2,1,0:T(8,128)(2,1)} %param.10) | copy-start | bytes 1572868
  7.2 196.0 %all-gather.2.cloned.1.call-start = ((), (), s32[]{:S(2)}) async-start(), calls=%async_computation.1 | async-start | bytes 2359296 | tf_op jit(solution)/shard_map/all_gather | solution.py:63
  7.2 18.2 %collective-permute-start = (bf16[1,512,512]{2,1,0:T(8,128)(2,1)}, bf16[1,512,512]{2,1,0:T(8,128)(2,1)S(1)}, u32[]{:S(2)}, u32[]{:S(2)}) collective-permute-start(bf16[1,512,512]{2,1,0:T(8,128)(2,1)} %param.10), channel_id=1, source_target_pairs={{0,1},{1,2},{2,3},{3,4},{4,5},{5,6},{6,7},{7,0},{8,9},{9,10},{10,1... | collective-permute-start | bytes 1572872 | tf_op jit(solution)/shard_map/ppermute | solution.py:50
  25.4 22.1 %collective-permute-start.1 = (bf16[1,512,512]{2,1,0:T(8,128)(2,1)S(1)}, bf16[1,512,512]{2,1,0:T(8,128)(2,1)S(1)}, u32[]{:S(2)}, u32[]{:S(2)}) collective-permute-start(bf16[1,512,512]{2,1,0:T(8,128)(2,1)S(1)} %collective-permute-done), channel_id=1, source_target_pairs={{0,1},{1,2},{2,3},{3,4},{4,5},{5,6},{6,7},{7,0},{8,9},{9,10},{10,1... | collective-permute-start | bytes 1572872 | tf_op jit(solution)/shard_map/ppermute | solution.py:50
  25.4 24.6 %collective-permute-start.4 = (bf16[1,512,512]{2,1,0:T(8,128)(2,1)}, bf16[1,512,512]{2,1,0:T(8,128)(2,1)S(1)}, u32[]{:S(2)}, u32[]{:S(2)}) collective-permute-start(bf16[1,512,512]{2,1,0:T(8,128)(2,1)} %param.10), channel_id=1, source_target_pairs={{0,7},{1,0},{2,1},{3,2},{4,3},{5,4},{6,5},{7,6},{8,15},{9,8},{10,9... | collective-permute-start | bytes 1572872 | tf_op jit(solution)/shard_map/ppermute | solution.py:51
  47.5 23.7 %collective-permute-start.2 = (bf16[1,512,512]{2,1,0:T(8,128)(2,1)S(1)}, bf16[1,512,512]{2,1,0:T(8,128)(2,1)}, u32[]{:S(2)}, u32[]{:S(2)}) collective-permute-start(bf16[1,512,512]{2,1,0:T(8,128)(2,1)S(1)} %collective-permute-done.1), channel_id=1, source_target_pairs={{0,1},{1,2},{2,3},{3,4},{4,5},{5,6},{6,7},{7,0},{8,9},{9,10},{10,1... | collective-permute-start | bytes 1572872 | tf_op jit(solution)/shard_map/ppermute | solution.py:50
  50.0 32.8 %collective-permute-start.5 = (bf16[1,512,512]{2,1,0:T(8,128)(2,1)S(1)}, bf16[1,512,512]{2,1,0:T(8,128)(2,1)S(1)}, u32[]{:S(2)}, u32[]{:S(2)}) collective-permute-start(bf16[1,512,512]{2,1,0:T(8,128)(2,1)S(1)} %collective-permute-done.4), channel_id=1, source_target_pairs={{0,7},{1,0},{2,1},{3,2},{4,3},{5,4},{6,5},{7,6},{8,15},{9,8},{10,9... | collective-permute-start | bytes 1572872 | tf_op jit(solution)/shard_map/ppermute | solution.py:51
  71.3 24.4 %collective-permute-start.3 = (bf16[1,512,512]{2,1,0:T(8,128)(2,1)}, bf16[1,512,512]{2,1,0:T(8,128)(2,1)}, u32[]{:S(2)}, u32[]{:S(2)}) collective-permute-start(bf16[1,512,512]{2,1,0:T(8,128)(2,1)} %collective-permute-done.2), channel_id=1, source_target_pairs={{0,1},{1,2},{2,3},{3,4},{4,5},{5,6},{6,7},{7,0},{8,9},{9,10},{10,1... | collective-permute-start | bytes 1572872 | tf_op jit(solution)/shard_map/ppermute | solution.py:50
  82.9 25.2 %collective-permute-start.6 = (bf16[1,512,512]{2,1,0:T(8,128)(2,1)S(1)}, bf16[1,512,512]{2,1,0:T(8,128)(2,1)S(1)}, u32[]{:S(2)}, u32[]{:S(2)}) collective-permute-start(bf16[1,512,512]{2,1,0:T(8,128)(2,1)S(1)} %collective-permute-done.5), channel_id=1, source_target_pairs={{0,7},{1,0},{2,1},{3,2},{4,3},{5,4},{6,5},{7,6},{8,15},{9,8},{10,9... | collective-permute-start | bytes 1572872 | tf_op jit(solution)/shard_map/ppermute | solution.py:51
  129.3 25.6 %copy-start.3 = (f32[512,512]{1,0:T(8,128)S(1)}, f32[512,512]{1,0:T(8,128)}, u32[]{:S(2)}) copy-start(f32[512,512]{1,0:T(8,128)} %param.13) | copy-start | bytes 3145732
  129.3 26.9 %copy-start.6 = (s32[512]{0:T(512)S(1)}, s32[512]{0:T(512)}, u32[]{:S(2)}) copy-start(s32[512]{0:T(512)} %param.12) | copy-start | bytes 6148
  129.3 26.9 %copy-start.8 = (s32[2]{0:T(128)S(1)}, s32[2]{0:T(128)}, u32[]{:S(2)}) copy-start(s32[2]{0:T(128)} %param.15) | copy-start | bytes 28
  129.3 77.7 %copy-start.7 = (f32[512]{0:T(512)S(1)}, f32[512]{0:T(512)}, u32[]{:S(2)}) copy-start(f32[512]{0:T(512)} %param.14) | copy-start | bytes 6148
  129.3 13.6 %collective-permute-start.7 = (f32[512,4096]{0,1:T(8,128)}, f32[512,4096]{0,1:T(8,128)}, u32[]{:S(2)}, u32[]{:S(2)}) collective-permute-start(f32[512,4096]{0,1:T(8,128)} %bitcast_subtract_fusion), channel_id=1, source_target_pairs={{0,8},{8,0},{16,24},{24,16},{1,9},{9,1},{17,25},{25,17},{2,10},{10... | collective-permute-start | bytes 25165832 | tf_op jit(solution)/shard_map/ppermute | solution.py:17
  154.0 182.8 %collective-permute-start.8 = (f32[512,4096]{0,1:T(8,128)}, f32[512,4096]{0,1:T(8,128)}, u32[]{:S(2)}, u32[]{:S(2)}) collective-permute-start(f32[512,4096]{0,1:T(8,128)} %add.48), channel_id=1, source_target_pairs={{0,16},{16,0},{8,24},{24,8},{1,17},{17,1},{9,25},{25,9},{2,18},{18... | collective-permute-start | bytes 25165832 | tf_op jit(solution)/shard_map/ppermute | solution.py:17
  154.6 263.4 %reduce-scatter.4.cloned.1.call-start = ((), (), s32[]{:S(2)}) async-start(), calls=%async_computation.2 | async-start | bytes 147456 | tf_op jit(solution)/shard_map/reduce_scatter | solution.py:81
  203.2 144.7 %copy-start.2 = (bf16[4096,256]{1,0:T(8,128)(2,1)S(1)}, bf16[4096,256]{1,0:T(8,128)(2,1)}, u32[]{:S(2)}) copy-start(bf16[4096,256]{1,0:T(8,128)(2,1)} %all-gather.2.cloned.1.call-done) | copy-start | bytes 6291460
  210.5 209.0 %copy-start.1 = (bf16[1,512,512]{2,1,0:T(8,128)(2,1)S(1)}, bf16[1,512,512]{2,1,0:T(8,128)(2,1)}, u32[]{:S(2)}) copy-start(bf16[1,512,512]{2,1,0:T(8,128)(2,1)} %param.9) | copy-start | bytes 1572868
  211.1 146.4 %copy-start.4 = (bf16[512,256]{1,0:T(8,128)(2,1)S(1)}, bf16[512,256]{1,0:T(8,128)(2,1)}, u32[]{:S(2)}) copy-start(bf16[512,256]{1,0:T(8,128)(2,1)} %param.11) | copy-start | bytes 786436
Sparse Core Ops, SparseCore 0:
  154.7 48.4 all-gather.1
  358.8 59.1 reduce-scatter.3
